TPU v7x, 32 devices: a whole 2x2x4 slice. The times are simulated.
32 devices in a mesh: section: 2 (over core), ctx: 4 (over y, x), dp: 4 (over z).
Axes of the slice: x: 2, y: 2, z: 4, core: 2. Of those that a mesh axis runs over, the one named last changes fastest.
Arguments:
- block_input: float32 [2, 4, 512, 960], P(None, 'dp', 'ctx'), may hold values from -6 to 6
- out_grad: float32 [2, 4, 512, 960], P(None, 'dp', 'ctx'), may hold values from -6 to 6
- w_query: bfloat16 [2, 960, 960], P('section', 'dp'), may hold values from -0.1875 to 0.1875
- w_key: bfloat16 [2, 960, 320], P('section', 'dp'), may hold values from -0.1875 to 0.1875
- w_value: bfloat16 [2, 960, 320], P('section', 'dp'), may hold values from -0.1875 to 0.1875
- w_out: bfloat16 [2, 960, 960], P('section', 'dp'), may hold values from -1.5 to 1.5
- norm_attn: bfloat16 [2, 960], P('section', 'dp'), may hold values from 0.099609375 to 1.8984375
- w_gate: bfloat16 [2, 960, 2560], P('section', None, 'dp'), may hold values from -0.1875 to 0.1875
- w_up: bfloat16 [2, 960, 2560], P('section', None, 'dp'), may hold values from -0.1875 to 0.1875
- w_down: bfloat16 [2, 2560, 960], P('section', 'dp'), may hold values from -0.125 to 0.125
- norm_ffn: bfloat16 [2, 960], P('section', 'dp'), may hold values from 0.099609375 to 1.8984375
Outputs:
- section_out: float32 [2, 2, 4, 512, 960], P('section', None, 'dp', 'ctx')
- section_in_grad: float32 [2, 2, 4, 512, 960], P('section', None, 'dp', 'ctx')
- grad_query: float32 [2, 960, 960], P('section', 'dp')
- grad_key: float32 [2, 960, 320], P('section', 'dp')
- grad_value: float32 [2, 960, 320], P('section', 'dp')
- grad_out: float32 [2, 960, 960], P('section', 'dp')
- grad_norm_attn: float32 [2, 960], P('section', 'dp')
- grad_gate: float32 [2, 960, 2560], P('section', None, 'dp')
- grad_up: float32 [2, 960, 2560], P('section', None, 'dp')
- grad_down: float32 [2, 2560, 960], P('section', 'dp')
- grad_norm_ffn: float32 [2, 960], P('section', 'dp')
All inputs are finite; a program needn't handle non-finite values.
Results may differ from a plain program's by a relative error of at most 0.03.
Values may be sent and summed in bfloat16 or wider, within the bound.
No kernel may reach another device: no remote copies, remote signals or barrier semaphores. Data moves between devices by JAX's collectives and lax.ppermute only.
A program may use at most 256 MiB of HBM per device.

v0:
```python
import jax
import jax.numpy as jnp
from jax import lax
from jax.sharding import PartitionSpec as P

D = 960
HEADS = 15
KV_HEADS = 5
HEAD_DIM = 64
QW = 960
KVW = 320
GROUP = 3


EPSILON = 1e-05
ROPE_BASE = 10000.0
MASKED = -1e30


def from_behind(block, axis, distance):
    devices = range(lax.axis_size(axis))
    route = [(i - distance, i) for i in devices if i - distance in devices]
    return lax.ppermute(block, axis, route)


def rope_tables(positions):
    half_dim = HEAD_DIM // 2
    freq_rows = ROPE_BASE ** (-(jnp.arange(half_dim, dtype=jnp.float32) * 2.0 / HEAD_DIM))
    angles = positions.astype(jnp.float32)[:, None] * freq_rows[None, :]
    cosine = jnp.concatenate([jnp.cos(angles), jnp.cos(angles)], axis=1)
    sine_rows = jnp.concatenate([jnp.sin(angles), jnp.sin(angles)], axis=1)
    return (cosine, sine_rows)


def turn_half(new_value):
    half_dim = HEAD_DIM // 2
    return jnp.concatenate([-new_value[..., half_dim:], new_value[..., :half_dim]], axis=-1)


def rotate(new_value, cosine, sine_rows):
    return new_value * cosine[:, None, :] + turn_half(new_value) * sine_rows[:, None, :]


def unrotate(grad_rows, cosine, sine_rows):
    return grad_rows * cosine[:, None, :] - turn_half(grad_rows * sine_rows[:, None, :])


def normalize(new_value, gain_row):
    inverse = lax.rsqrt(jnp.mean(new_value * new_value, axis=-1, keepdims=True) + EPSILON)
    return (new_value * inverse * gain_row.astype(jnp.float32), inverse)


def normalize_back(new_value, inverse, gain_row, grad_rows):
    scaled = grad_rows * gain_row.astype(jnp.float32)
    gain_grad = jnp.sum(grad_rows * new_value * inverse, axis=0)
    value_grad = inverse * scaled - new_value * inverse**3 * jnp.mean(
        scaled * new_value, axis=-1, keepdims=True
    )
    return (value_grad, gain_grad)


def project(normed, wq_all, wk_all, wv_all, cosine, sine_rows):
    row_count = normed.shape[0]
    queries = jnp.dot(normed, wq_all, preferred_element_type=jnp.float32).reshape(
        row_count, HEADS, HEAD_DIM
    )
    queries = (
        rotate(queries, cosine, sine_rows)
        .astype(jnp.bfloat16)
        .reshape(row_count, KV_HEADS, GROUP, HEAD_DIM)
    )
    key_rows = jnp.dot(normed, wk_all, preferred_element_type=jnp.float32).reshape(
        row_count, KV_HEADS, HEAD_DIM
    )
    key_rows = rotate(key_rows, cosine, sine_rows).astype(jnp.bfloat16).reshape(row_count, KVW)
    value_rows = jnp.dot(normed, wv_all, preferred_element_type=jnp.float32).astype(jnp.bfloat16)
    return (queries, key_rows, value_rows)


def store_slot(buffer, new_value, slot_id, is_valid):
    current = lax.dynamic_index_in_dim(buffer, slot_id, 0, keepdims=False)
    chosen = jnp.where(is_valid, new_value, current)
    return lax.dynamic_update_index_in_dim(buffer, chosen, slot_id, 0)


def load_slot(buffer, slot_id):
    return lax.dynamic_index_in_dim(buffer, slot_id, 0, keepdims=False)


def gather_keys(key_rows, value_rows):
    return (
        lax.all_gather(key_rows, "ctx", axis=0, tiled=True),
        lax.all_gather(value_rows, "ctx", axis=0, tiled=True),
    )


def head_columns(per_head, tok_rows):
    return jnp.repeat(per_head.reshape(HEADS, tok_rows).T, HEAD_DIM, axis=1)


def block_count(query_pos, first_row, key_span, row_count):
    reach = (query_pos[-1] - first_row) // key_span + 1
    return jnp.clip(reach, 0, row_count // key_span)


def attend_rows(state_in, key_rows, value_rows, first_row, queries, query_pos):
    row_count = key_rows.shape[0]
    key_span = 512 if row_count > 512 and row_count % 512 == 0 else row_count
    score_scale = HEAD_DIM ** (-0.5)
    tok_rows = queries.shape[0]

    def attend_one_block(block_id, loop_state):
        run_peak, denom_sum, mixture = loop_state
        offset = block_id * key_span
        key_block = lax.dynamic_slice_in_dim(key_rows, offset, key_span, 0).reshape(
            key_span, KV_HEADS, HEAD_DIM
        )
        value_block = lax.dynamic_slice_in_dim(value_rows, offset, key_span, 0).reshape(
            key_span, KV_HEADS, HEAD_DIM
        )
        scores = (
            jnp.einsum("tkgd,skd->kgts", queries, key_block, preferred_element_type=jnp.float32)
            * score_scale
        )
        key_pos = offset + jnp.arange(key_span, dtype=jnp.int32)
        allowed = query_pos[:, None] >= key_pos[None, :]
        new_peak = jnp.maximum(run_peak, jnp.max(jnp.where(allowed, scores, MASKED), axis=-1))
        weights = jnp.where(allowed, jnp.exp(scores - new_peak[..., None]), 0.0)
        rescale = jnp.exp(run_peak - new_peak)
        denom_sum = denom_sum * rescale + jnp.sum(weights, axis=-1)
        update = jnp.einsum(
            "kgts,skd->tkgd",
            weights,
            value_block.astype(jnp.float32),
            precision=lax.Precision.HIGHEST,
            preferred_element_type=jnp.float32,
        )
        mixture = mixture * head_columns(rescale, tok_rows) + update.reshape(tok_rows, QW)
        return (new_peak, denom_sum, mixture)

    limit = block_count(query_pos, first_row, key_span, row_count)
    return lax.fori_loop(0, limit, attend_one_block, state_in)


def attention_back(key_rows, value_rows, queries, grad_mix, log_totals, row_delta, query_pos):
    seq_rows = key_rows.shape[0]
    key_span = min(512, seq_rows)
    score_scale = HEAD_DIM ** (-0.5)
    tok_rows = queries.shape[0]

    def attention_one_block(block_id, loop_state):
        query_grad, kv_grad = loop_state
        offset = block_id * key_span
        key_block = lax.dynamic_slice_in_dim(key_rows, offset, key_span, 0).reshape(
            key_span, KV_HEADS, HEAD_DIM
        )
        value_block = lax.dynamic_slice_in_dim(value_rows, offset, key_span, 0).reshape(
            key_span, KV_HEADS, HEAD_DIM
        )
        scores = (
            jnp.einsum("tkgd,skd->kgts", queries, key_block, preferred_element_type=jnp.float32)
            * score_scale
        )
        key_pos = offset + jnp.arange(key_span, dtype=jnp.int32)
        allowed = query_pos[:, None] >= key_pos[None, :]
        prob_rows = jnp.where(allowed, jnp.exp(scores - log_totals[..., None]), 0.0)
        value_part = jnp.einsum(
            "kgts,tkgd->skd",
            prob_rows.astype(jnp.bfloat16),
            grad_mix,
            preferred_element_type=jnp.float32,
        )
        prob_grad = jnp.einsum(
            "tkgd,skd->kgts", grad_mix, value_block, preferred_element_type=jnp.float32
        )
        score_grad = (prob_rows * (prob_grad - row_delta[..., None])).astype(jnp.bfloat16)
        query_part = jnp.einsum(
            "kgts,skd->tkgd", score_grad, key_block, preferred_element_type=jnp.float32
        )
        query_grad = query_grad + query_part.reshape(tok_rows, QW) * score_scale
        key_part = (
            jnp.einsum("kgts,tkgd->skd", score_grad, queries, preferred_element_type=jnp.float32)
            * score_scale
        )
        joined = jnp.concatenate(
            [key_part.reshape(key_span, KVW), value_part.reshape(key_span, KVW)], axis=1
        )
        kv_grad = lax.dynamic_update_slice_in_dim(kv_grad, joined, offset, 0)
        return (query_grad, kv_grad)

    start_state = (
        jnp.zeros((tok_rows, QW), jnp.float32),
        jnp.zeros((seq_rows, 2 * KVW), jnp.float32),
    )
    limit = block_count(query_pos, 0, key_span, seq_rows)
    return lax.fori_loop(0, limit, attention_one_block, start_state)


def body(
    block_input, out_grad, w_query, w_key, w_value, w_out, norm_attn, w_gate, w_up, w_down, norm_ffn
):
    section_count = lax.axis_size("section")
    section_id = lax.axis_index("section")
    last_section = section_count - 1
    micro_count = block_input.shape[0]
    tok_rows = block_input.shape[2]
    query_pos = lax.axis_index("ctx") * tok_rows + jnp.arange(tok_rows, dtype=jnp.int32)
    cosine, sine_rows = rope_tables(query_pos)
    local_in = block_input[:, 0]
    local_grad = out_grad[:, 0]
    wq_all, wk_all, wv_all, wo_all, gain_attn, gain_ffn = (
        lax.all_gather(w_query[0], "dp", axis=0, tiled=True),
        lax.all_gather(w_key[0], "dp", axis=0, tiled=True),
        lax.all_gather(w_value[0], "dp", axis=0, tiled=True),
        lax.all_gather(w_out[0], "dp", axis=0, tiled=True),
        lax.all_gather(norm_attn[0], "dp", axis=0, tiled=True),
        lax.all_gather(norm_ffn[0], "dp", axis=0, tiled=True),
    )
    wg_use, wu_use, wd_use = (
        lax.all_gather(w_gate[0], "dp", axis=1, tiled=True),
        lax.all_gather(w_up[0], "dp", axis=1, tiled=True),
        lax.all_gather(w_down[0], "dp", axis=0, tiled=True),
    )
    tick_count = micro_count + section_count - 1
    saved_in = jnp.zeros((micro_count, tok_rows, D), jnp.float32)
    saved_mix = jnp.zeros((micro_count, tok_rows, QW), jnp.bfloat16)
    saved_lse = jnp.zeros((micro_count, KV_HEADS, GROUP, tok_rows), jnp.float32)
    section_outs = jnp.zeros((micro_count, tok_rows, D), jnp.float32)
    received = jnp.zeros((tok_rows, D), jnp.float32)
    for tick_id in range(tick_count):
        micro_id = tick_id - section_id
        is_valid = (micro_id >= 0) & (micro_id < micro_count)
        slot_id = jnp.clip(micro_id, 0, micro_count - 1)
        layer_in = jnp.where(section_id == 0, load_slot(local_in, slot_id), received)
        normed_a, inverse_a = normalize(layer_in, gain_attn)
        normed_a = normed_a.astype(jnp.bfloat16)
        queries, key_rows, value_rows = project(normed_a, wq_all, wk_all, wv_all, cosine, sine_rows)
        start_state = (
            jnp.full((KV_HEADS, GROUP, tok_rows), MASKED, jnp.float32),
            jnp.zeros((KV_HEADS, GROUP, tok_rows), jnp.float32),
            jnp.zeros((tok_rows, QW), jnp.float32),
        )
        run_peak, denom_sum, mixture = attend_rows(
            start_state,
            lax.all_gather(key_rows, "ctx", axis=0, tiled=True),
            lax.all_gather(value_rows, "ctx", axis=0, tiled=True),
            jnp.int32(0),
            queries,
            query_pos,
        )
        mixture = (mixture / head_columns(denom_sum, tok_rows)).astype(jnp.bfloat16)
        log_totals = run_peak + jnp.log(denom_sum)
        after_attn = layer_in + jnp.dot(mixture, wo_all, preferred_element_type=jnp.float32)
        normed_f, inverse_f = normalize(after_attn, gain_ffn)
        normed_f = normed_f.astype(jnp.bfloat16)
        gate_pre = jnp.dot(normed_f, wg_use, preferred_element_type=jnp.float32)
        up_proj = jnp.dot(normed_f, wu_use, preferred_element_type=jnp.float32)
        hidden = (jax.nn.silu(gate_pre) * up_proj).astype(jnp.bfloat16)
        layer_out = after_attn + jnp.dot(hidden, wd_use, preferred_element_type=jnp.float32)
        saved_in = store_slot(saved_in, layer_in, slot_id, is_valid)
        saved_mix = store_slot(saved_mix, mixture, slot_id, is_valid)
        saved_lse = store_slot(saved_lse, log_totals, slot_id, is_valid)
        section_outs = store_slot(section_outs, layer_out, slot_id, is_valid)
        if tick_id < tick_count - 1:
            received = from_behind(layer_out.astype(jnp.bfloat16), "section", 1).astype(
                layer_out.dtype
            )
    acc_query = jnp.zeros(wq_all.shape, jnp.float32)
    acc_key = jnp.zeros(wk_all.shape, jnp.float32)
    acc_value = jnp.zeros(wv_all.shape, jnp.float32)
    acc_out = jnp.zeros(wo_all.shape, jnp.float32)
    acc_gain_a = jnp.zeros((D,), jnp.float32)
    acc_gate = jnp.zeros(wg_use.shape, jnp.float32)
    acc_up = jnp.zeros(wu_use.shape, jnp.float32)
    acc_down = jnp.zeros(wd_use.shape, jnp.float32)
    acc_gain_f = jnp.zeros((D,), jnp.float32)
    in_grads = jnp.zeros((micro_count, tok_rows, D), jnp.float32)
    received = jnp.zeros((tok_rows, D), jnp.float32)
    for tick_id in range(tick_count):
        micro_id = tick_id - (last_section - section_id)
        is_valid = (micro_id >= 0) & (micro_id < micro_count)
        slot_id = jnp.clip(micro_id, 0, micro_count - 1)
        incoming = jnp.where(section_id == last_section, load_slot(local_grad, slot_id), received)
        incoming = jnp.where(is_valid, incoming, 0.0)
        layer_in = load_slot(saved_in, slot_id)
        mixture = load_slot(saved_mix, slot_id)
        log_totals = load_slot(saved_lse, slot_id)
        normed_a, inverse_a = normalize(layer_in, gain_attn)
        normed_a = normed_a.astype(jnp.bfloat16)
        queries, key_rows, value_rows = project(normed_a, wq_all, wk_all, wv_all, cosine, sine_rows)
        after_attn = layer_in + jnp.dot(mixture, wo_all, preferred_element_type=jnp.float32)
        normed_f, inverse_f = normalize(after_attn, gain_ffn)
        normed_f = normed_f.astype(jnp.bfloat16)
        grad_b = incoming.astype(jnp.bfloat16)
        gate_pre = jnp.dot(normed_f, wg_use, preferred_element_type=jnp.float32)
        up_proj = jnp.dot(normed_f, wu_use, preferred_element_type=jnp.float32)
        hidden = (jax.nn.silu(gate_pre) * up_proj).astype(jnp.bfloat16)
        acc_down = acc_down + jnp.dot(hidden.T, grad_b, preferred_element_type=jnp.float32)
        hidden_grad = jnp.dot(grad_b, wd_use.T, preferred_element_type=jnp.float32)
        sigma_gate = jax.nn.sigmoid(gate_pre)
        gate_grad = (
            hidden_grad * up_proj * sigma_gate * (1.0 + gate_pre * (1.0 - sigma_gate))
        ).astype(jnp.bfloat16)
        up_grad = (hidden_grad * gate_pre * sigma_gate).astype(jnp.bfloat16)
        acc_gate = acc_gate + jnp.dot(normed_f.T, gate_grad, preferred_element_type=jnp.float32)
        acc_up = acc_up + jnp.dot(normed_f.T, up_grad, preferred_element_type=jnp.float32)
        normed_grad = jnp.dot(gate_grad, wg_use.T, preferred_element_type=jnp.float32) + jnp.dot(
            up_grad, wu_use.T, preferred_element_type=jnp.float32
        )
        back_f, gain_part = normalize_back(after_attn, inverse_f, gain_ffn, normed_grad)
        acc_gain_f = acc_gain_f + gain_part
        attn_grad = incoming + back_f
        attn_b = attn_grad.astype(jnp.bfloat16)
        acc_out = acc_out + jnp.dot(mixture.T, attn_b, preferred_element_type=jnp.float32)
        mix_grad = jnp.dot(attn_b, wo_all.T, preferred_element_type=jnp.float32).astype(
            jnp.bfloat16
        )
        row_delta = jnp.sum(
            (mix_grad.astype(jnp.float32) * mixture.astype(jnp.float32)).reshape(
                tok_rows, KV_HEADS, GROUP, HEAD_DIM
            ),
            axis=-1,
        )
        row_delta = jnp.transpose(row_delta, (1, 2, 0))
        key_all, value_all = gather_keys(key_rows, value_rows)
        query_grad, kv_grad = attention_back(
            key_all,
            value_all,
            queries,
            mix_grad.reshape(tok_rows, KV_HEADS, GROUP, HEAD_DIM),
            log_totals,
            row_delta,
            query_pos,
        )
        own_kv = lax.psum_scatter(
            kv_grad.astype(jnp.bfloat16), "ctx", scatter_dimension=0, tiled=True
        ).astype(jnp.float32)
        query_b = (
            unrotate(query_grad.reshape(tok_rows, HEADS, HEAD_DIM), cosine, sine_rows)
            .reshape(tok_rows, QW)
            .astype(jnp.bfloat16)
        )
        key_b = (
            unrotate(own_kv[:, :KVW].reshape(tok_rows, KV_HEADS, HEAD_DIM), cosine, sine_rows)
            .reshape(tok_rows, KVW)
            .astype(jnp.bfloat16)
        )
        value_b = own_kv[:, KVW:].astype(jnp.bfloat16)
        acc_query = acc_query + jnp.dot(normed_a.T, query_b, preferred_element_type=jnp.float32)
        acc_key = acc_key + jnp.dot(normed_a.T, key_b, preferred_element_type=jnp.float32)
        acc_value = acc_value + jnp.dot(normed_a.T, value_b, preferred_element_type=jnp.float32)
        normed_grad_a = (
            jnp.dot(query_b, wq_all.T, preferred_element_type=jnp.float32)
            + jnp.dot(key_b, wk_all.T, preferred_element_type=jnp.float32)
            + jnp.dot(value_b, wv_all.T, preferred_element_type=jnp.float32)
        )
        back_a, gain_part = normalize_back(layer_in, inverse_a, gain_attn, normed_grad_a)
        acc_gain_a = acc_gain_a + gain_part
        layer_grad = attn_grad + back_a
        in_grads = store_slot(in_grads, layer_grad, slot_id, is_valid)
        if tick_id < tick_count - 1:
            received = from_behind(layer_grad.astype(jnp.bfloat16), "section", -1).astype(
                layer_grad.dtype
            )
    shards = (
        lax.psum_scatter(
            acc_query.astype(jnp.bfloat16), "dp", scatter_dimension=0, tiled=True
        ).astype(jnp.float32),
        lax.psum_scatter(
            acc_key.astype(jnp.bfloat16), "dp", scatter_dimension=0, tiled=True
        ).astype(jnp.float32),
        lax.psum_scatter(
            acc_value.astype(jnp.bfloat16), "dp", scatter_dimension=0, tiled=True
        ).astype(jnp.float32),
        lax.psum_scatter(
            acc_out.astype(jnp.bfloat16), "dp", scatter_dimension=0, tiled=True
        ).astype(jnp.float32),
        lax.psum_scatter(
            acc_gain_a.astype(jnp.bfloat16), "dp", scatter_dimension=0, tiled=True
        ).astype(jnp.float32),
        lax.psum_scatter(
            acc_gate.astype(jnp.bfloat16), "dp", scatter_dimension=1, tiled=True
        ).astype(jnp.float32),
        lax.psum_scatter(acc_up.astype(jnp.bfloat16), "dp", scatter_dimension=1, tiled=True).astype(
            jnp.float32
        ),
        lax.psum_scatter(
            acc_down.astype(jnp.bfloat16), "dp", scatter_dimension=0, tiled=True
        ).astype(jnp.float32),
        lax.psum_scatter(
            acc_gain_f.astype(jnp.bfloat16), "dp", scatter_dimension=0, tiled=True
        ).astype(jnp.float32),
    )
    totals = (
        lax.psum(shards[0].astype(jnp.bfloat16), "ctx").astype(jnp.float32),
        lax.psum(shards[1].astype(jnp.bfloat16), "ctx").astype(jnp.float32),
        lax.psum(shards[2].astype(jnp.bfloat16), "ctx").astype(jnp.float32),
        lax.psum(shards[3].astype(jnp.bfloat16), "ctx").astype(jnp.float32),
        lax.psum(shards[4].astype(jnp.bfloat16), "ctx").astype(jnp.float32),
        lax.psum(shards[5].astype(jnp.bfloat16), "ctx").astype(jnp.float32),
        lax.psum(shards[6].astype(jnp.bfloat16), "ctx").astype(jnp.float32),
        lax.psum(shards[7].astype(jnp.bfloat16), "ctx").astype(jnp.float32),
        lax.psum(shards[8].astype(jnp.bfloat16), "ctx").astype(jnp.float32),
    )
    return (
        section_outs[None, :, None],
        in_grads[None, :, None],
        totals[0][None],
        totals[1][None],
        totals[2][None],
        totals[3][None],
        totals[4][None],
        totals[5][None],
        totals[6][None],
        totals[7][None],
        totals[8][None],
    )


def solution(mesh):
    return jax.shard_map(
        body,
        mesh=mesh,
        in_specs=(
            P(None, "dp", "ctx", None),
            P(None, "dp", "ctx", None),
            P("section", "dp", None),
            P("section", "dp", None),
            P("section", "dp", None),
            P("section", "dp", None),
            P("section", "dp"),
            P("section", None, "dp"),
            P("section", None, "dp"),
            P("section", "dp", None),
            P("section", "dp"),
        ),
        out_specs=(
            P("section", None, "dp", "ctx", None),
            P("section", None, "dp", "ctx", None),
            P("section", "dp", None),
            P("section", "dp", None),
            P("section", "dp", None),
            P("section", "dp", None),
            P("section", "dp"),
            P("section", None, "dp"),
            P("section", None, "dp"),
            P("section", "dp", None),
            P("section", "dp"),
        ),
        check_vma=False,
    )
```

profile of v0, /device:TPU:0, one launch (start us, length us, event | category | flops | bytes accessed | tf_op | source)
XLA Modules:
  0.0 1353.7 jit_solution(18270609059686976154)
XLA Ops:
  14.7 53.7 %all-gather.1 = bf16[1,960,320]{2,0,1:T(2,128)(2,1)} all-gather(bf16[1,240,320]{2,0,1:T(2,128)(2,1)S(1)} %copy.67), channel_id=3, replica_groups=mesh['section'=2,'ctx'=4,'dp'=4] {'dp'}, dimensions={1}, use_global_device_ids=true | all-gather | bytes 768000 | tf_op jit(solution)/shard_map/all_gather | solution.py:213
  73.8 12.6 all-reduce.5
  87.3 9.8 all_gather.65
  97.8 47.1 %all-gather.3 = bf16[1,960,320]{2,0,1:T(2,128)(2,1)} all-gather(bf16[1,240,320]{2,0,1:T(2,128)(2,1)S(1)} %copy.70), channel_id=5, replica_groups=mesh['section'=2,'ctx'=4,'dp'=4] {'dp'}, dimensions={1}, use_global_device_ids=true | all-gather | bytes 768000 | tf_op jit(solution)/shard_map/all_gather | solution.py:214
  149.0 10.0 all_gather.68
  167.8 8.1 while.84
  182.7 54.6 %all-gather.19.cloned.1.call-done = bf16[1,960,2560]{2,1,0:T(8,128)(2,1)} async-done(((bf16[1,960,640]{2,1,0:T(8,128)(2,1)}), bf16[1,960,2560]{2,1,0:T(8,128)(2,1)}) %all-gather.19.cloned.1.call-update) | async-done | bytes 4915216 | tf_op jit(solution)/shard_map/all_gather | solution.py:220
  241.9 87.9 %all-gather.23.cloned.1.call-done = bf16[1,2560,960]{1,2,0:T(8,128)(2,1)} async-done(((bf16[1,640,960]{1,2,0:T(8,128)(2,1)}), bf16[1,2560,960]{1,2,0:T(8,128)(2,1)}) %all-gather.23.cloned.1.call-update) | async-done | bytes 4915216 | tf_op jit(solution)/shard_map/all_gather | solution.py:222
  329.8 92.5 %all-gather.21.cloned.1.call-done = bf16[1,960,2560]{2,1,0:T(8,128)(2,1)} async-done(((bf16[1,960,640]{2,1,0:T(8,128)(2,1)}), bf16[1,960,2560]{2,1,0:T(8,128)(2,1)}) %all-gather.21.cloned.1.call-update) | async-done | bytes 4915216 | tf_op jit(solution)/shard_map/all_gather | solution.py:221
  423.3 7.6 bitcast_dynamic-update-slice_fusion.7
  439.2 9.9 all_gather.74
  450.1 9.8 all_gather.75
  461.3 8.8 while.85
  479.9 7.8 bitcast_dynamic-update-slice_fusion.6
  499.7 9.2 all_gather.76
  509.9 9.5 all_gather.77
  520.3 7.3 while.86
  546.1 8.9 all_gather.78
  556.1 9.8 all_gather.79
  571.1 12.5 while.87
  596.7 12.5 reduce-scatter.31.cloned.1.call-done
  620.8 9.8 all_gather.80
  631.0 9.2 all_gather.81
  653.2 12.3 while.88
  678.2 15.4 %reduce-scatter.33.cloned.1.call-done = bf16[128,640]{1,0:T(8,128)(2,1)} async-done(((bf16[512,640]{1,0:T(8,128)(2,1)}), bf16[128,640]{1,0:T(8,128)(2,1)}) %reduce-scatter.33.cloned.1.call-update) | async-done | bytes 163856
  703.9 10.1 all_gather.82
  714.4 9.0 all_gather.83
  736.4 12.5 while.89
  755.0 22.0 %reduce-scatter.35.cloned.1.call-done = bf16[128,640]{1,0:T(8,128)(2,1)} async-done(((bf16[512,640]{1,0:T(8,128)(2,1)}), bf16[128,640]{1,0:T(8,128)(2,1)}) %reduce-scatter.35.cloned.1.call-update) | async-done | bytes 163856
  787.5 6.3 fusion.463
  798.5 6.7 fusion.464
  805.2 7.8 add_convert_fusion.2
  813.1 7.8 copy.114
  823.7 5.1 fusion.466
  828.9 7.9 add_convert_fusion.1
  836.8 7.9 copy.116
  848.4 5.2 fusion.250
  853.6 6.5 add_convert_fusion
  860.1 7.9 copy.118
  881.9 49.0 %reduce-scatter.41.cloned.1.call-done = bf16[640,960]{1,0:T(8,128)(2,1)} async-done(((bf16[2560,960]{1,0:T(8,128)(2,1)}), bf16[640,960]{1,0:T(8,128)(2,1)}) %reduce-scatter.41.cloned.1.call-update) | async-done | bytes 1228816
  933.2 94.1 %reduce-scatter.43.cloned.1.call-done = bf16[640,960]{1,0:T(8,128)(2,1)} async-done(((bf16[2560,960]{1,0:T(8,128)(2,1)}), bf16[640,960]{1,0:T(8,128)(2,1)}) %reduce-scatter.43.cloned.1.call-update) | async-done | bytes 1228816
  1029.7 94.2 %reduce-scatter.45.cloned.1.call-done = bf16[640,960]{1,0:T(8,128)(2,1)} async-done(((bf16[2560,960]{1,0:T(8,128)(2,1)}), bf16[640,960]{1,0:T(8,128)(2,1)}) %reduce-scatter.45.cloned.1.call-update) | async-done | bytes 1228816
  1126.4 42.4 %reduce-scatter.27.cloned.1.call-done = bf16[240,960]{1,0:T(8,128)(2,1)} async-done(((bf16[960,960]{1,0:T(8,128)(2,1)}), bf16[240,960]{1,0:T(8,128)(2,1)}) %reduce-scatter.27.cloned.1.call-update) | async-done | bytes 460816 | tf_op jit(solution)/shard_map/reduce_scatter | solution.py:366
  1168.8 43.5 %reduce-scatter.29.cloned.1.call-done = bf16[240,960]{1,0:T(8,128)(2,1)} async-done(((bf16[960,960]{1,0:T(8,128)(2,1)}), bf16[240,960]{1,0:T(8,128)(2,1)}) %reduce-scatter.29.cloned.1.call-update) | async-done | bytes 460816 | tf_op jit(solution)/shard_map/reduce_scatter | solution.py:375
  1222.3 7.7 fusion.246
  1233.3 10.8 all-reduce.4
  1244.3 9.5 all-reduce.6
  1256.0 78.3 %all-reduce.10.cloned.1.call-done = (bf16[1,240,960]{2,1,0:T(8,128)(2,1)}, bf16[1,240,320]{1,2,0:T(8,128)(2,1)}, bf16[1,240,320]{1,2,0:T(8,128)(2,1)}, bf16[1,24...) async-done(((bf16[1,240,960]{2,1,0:T(8,128)(2,1)}, bf16[1,240,320]{1,2,0:T(8,128)(2,1)}, ...) | async-done | bytes 4915216 | tf_op jit(solution)/shard_map/psum | solution.py:395
  (756 shorter events, 303.4 us)
Async XLA Ops:
  7.2 152.8 %all-gather.15.cloned.1.call-start = ((), (), s32[]{:S(2)}) async-start(), calls=%async_computation.12 | async-start | bytes 2457600 | tf_op jit(solution)/shard_map/all_gather | solution.py:212
  7.9 171.5 %all-gather.17.cloned.1.call-start = ((), (), s32[]{:S(2)}) async-start(), calls=%async_computation.13 | async-start | bytes 2457600 | tf_op jit(solution)/shard_map/all_gather | solution.py:215
  8.7 63.3 %copy-start.179 = (bf16[1,240]{1,0:T(2,128)(2,1)S(1)}, bf16[1,240]{1,0:T(2,128)(2,1)}, u32[]{:S(2)}) copy-start(bf16[1,240]{1,0:T(2,128)(2,1)} %param.29) | copy-start | bytes 1444
  8.7 63.4 %copy-start.180 = (bf16[1,240]{1,0:T(2,128)(2,1)S(1)}, bf16[1,240]{1,0:T(2,128)(2,1)}, u32[]{:S(2)}) copy-start(bf16[1,240]{1,0:T(2,128)(2,1)} %param.33) | copy-start | bytes 1444
  8.7 63.4 %copy-start.178 = (u32[32]{0:T(128)S(1)}, u32[32]{0:T(128)}, u32[]{:S(2)}) copy-start(u32[32]{0:T(128)} %constant.293) | copy-start | bytes 388
  8.7 77.8 %copy-start.24 = (f32[2,1,128,960]{2,3,1,0:T(8,128)S(1)}, f32[2,1,128,960]{2,3,1,0:T(8,128)}, u32[]{:S(2)}) copy-start(f32[2,1,128,960]{2,3,1,0:T(8,128)} %param.23) | copy-start | bytes 2949124
  8.7 228.6 %all-gather.19.cloned.1.call-start = ((), (), s32[]{:S(2)}) async-start(), calls=%async_computation.14 | async-start | bytes 6144000 | tf_op jit(solution)/shard_map/all_gather | solution.py:220
  9.5 320.4 %all-gather.23.cloned.1.call-start = ((), (), s32[]{:S(2)}) async-start(), calls=%async_computation.16 | async-start | bytes 6144000 | tf_op jit(solution)/shard_map/all_gather | solution.py:222
  10.0 412.2 %all-gather.21.cloned.1.call-start = ((), (), s32[]{:S(2)}) async-start(), calls=%async_computation.15 | async-start | bytes 6144000 | tf_op jit(solution)/shard_map/all_gather | solution.py:221
  10.6 86.5 %copy-start.157 = (bf16[1,240,320]{1,2,0:T(8,128)(2,1)S(1)}, bf16[1,240,320]{1,2,0:T(8,128)(2,1)}, u32[]{:S(2)}) copy-start(bf16[1,240,320]{1,2,0:T(8,128)(2,1)} %param.27) | copy-start | bytes 460804
  10.6 598.6 %reduce-scatter.31.cloned.1.call-start = ((), (), s32[]{:S(2)}) async-start(), calls=%async_computation.17 | async-start | bytes 819200
  72.0 366.4 %copy-start.9 = (bf16[1,960,320]{1,2,0:T(8,128)(2,1)}, bf16[1,960,320]{1,2,0:T(8,128)(2,1)S(1)}, u32[]{:S(2)}) copy-start(bf16[1,960,320]{1,2,0:T(8,128)(2,1)S(1)} %copy.68) | copy-start | bytes 1843204
  86.5 410.9 %copy-start.118 = (f32[960]{0:T(1024)}, f32[960]{0:T(1024)S(1)}, u32[]{:S(2)}) copy-start(f32[960]{0:T(1024)S(1)} %convert_element_type.468) | copy-start | bytes 11524
  87.3 432.2 %copy-start.42 = (f32[128,64]{0,1:T(8,128)}, f32[128,64]{0,1:T(8,128)S(1)}, u32[]{:S(2)}) copy-start(f32[128,64]{0,1:T(8,128)S(1)} %pad_maximum_fusion.10) | copy-start | bytes 98308
  148.5 290.3 %copy-start.14 = (bf16[1,960,320]{1,2,0:T(8,128)(2,1)}, bf16[1,960,320]{1,2,0:T(8,128)(2,1)S(1)}, u32[]{:S(2)}) copy-start(bf16[1,960,320]{1,2,0:T(8,128)(2,1)S(1)} %copy.71) | copy-start | bytes 1843204
  159.0 264.3 %copy-start.141 = (f32[960]{0:T(1024)}, f32[960]{0:T(1024)S(1)}, u32[]{:S(2)}) copy-start(f32[960]{0:T(1024)S(1)} %convert_element_type.469) | copy-start | bytes 11524
  177.8 64.1 %copy-start.151 = (f32[2,5,3,128]{3,2,1,0:T(4,128)}, f32[2,5,3,128]{3,2,1,0:T(4,128)S(1)}, u32[]{:S(2)}) copy-start(f32[2,5,3,128]{3,2,1,0:T(4,128)S(1)} %bitcast_dynamic-update-slice_fusion.13) | copy-start | bytes 46084
  430.9 7.2 collective-permute-start
  487.7 5.5 collective-permute-start.1
  585.9 107.7 %reduce-scatter.33.cloned.1.call-start = ((), (), s32[]{:S(2)}) async-start(), calls=%async_computation.18 | async-start | bytes 819200
  618.1 22.1 %copy-start.45 = (f32[128,64]{0,1:T(8,128)S(1)}, f32[128,64]{0,1:T(8,128)}, u32[]{:S(2)}) copy-start(f32[128,64]{0,1:T(8,128)} %copy-done.42) | copy-start | bytes 98308
  618.1 22.3 %copy-start.66 = (f32[2,1,128,960]{2,3,1,0:T(8,128)S(1)}, f32[2,1,128,960]{2,3,1,0:T(8,128)}, u32[]{:S(2)}) copy-start(f32[2,1,128,960]{2,3,1,0:T(8,128)} %param.24) | copy-start | bytes 2949124
  618.1 22.3 %copy-start.90 = (f32[128,2560]{1,0:T(8,128)S(1)}, f32[128,2560]{1,0:T(8,128)}, u32[]{:S(2)}) copy-start(f32[128,2560]{1,0:T(8,128)} %fusion.117) | copy-start | bytes 3932164
  618.1 22.3 %copy-start.92 = (f32[128,2560]{1,0:T(8,128)S(1)}, f32[128,2560]{1,0:T(8,128)}, u32[]{:S(2)}) copy-start(f32[128,2560]{1,0:T(8,128)} %fusion.99) | copy-start | bytes 3932164
  618.1 27.7 %slice-start.2 = ((s8[4915200]{0:T(1024)(128)(4,1)}), s8[4194304]{0:T(1024)(128)(4,1)S(1)}, s32[]{:S(2)}) async-start(s8[4915200]{0:T(1024)(128)(4,1)} %bitcast.1123), calls=%async_computation.28 | async-start | bytes 8388608
  619.2 21.2 %collective-permute-start.2 = (bf16[128,960]{0,1:T(8,128)(2,1)S(1)}, bf16[128,960]{0,1:T(8,128)(2,1)S(1)}, u32[]{:S(2)}, u32[]{:S(2)}) collective-permute-start(bf16[128,960]{0,1:T(8,128)(2,1)S(1)} %get-tuple-element.679), channel_id=1, source_target_pairs={{16,0},{17,1},{18,2},{19,3},{20,4},{21,5},{22,6},{23,7},{24,8},{25... | collective-permute-start | bytes 737288 | tf_op jit(solution)/shard_map/ppermute | solution.py:23
  667.8 109.2 %reduce-scatter.35.cloned.1.call-start = ((), (), s32[]{:S(2)}) async-start(), calls=%async_computation.19 | async-start | bytes 819200
  701.3 22.1 %copy-start.47 = (f32[128,64]{0,1:T(8,128)S(1)}, f32[128,64]{0,1:T(8,128)}, u32[]{:S(2)}) copy-start(f32[128,64]{0,1:T(8,128)} %copy-done.42) | copy-start | bytes 98308
  701.3 22.2 %copy-start.67 = (f32[2,1,128,960]{2,3,1,0:T(8,128)S(1)}, f32[2,1,128,960]{2,3,1,0:T(8,128)}, u32[]{:S(2)}) copy-start(f32[2,1,128,960]{2,3,1,0:T(8,128)} %param.24) | copy-start | bytes 2949124
  701.4 22.2 %copy-start.85 = (f32[128,2560]{1,0:T(8,128)S(1)}, f32[128,2560]{1,0:T(8,128)}, u32[]{:S(2)}) copy-start(f32[128,2560]{1,0:T(8,128)} %fusion.113) | copy-start | bytes 3932164
  701.4 22.2 %copy-start.87 = (f32[128,2560]{1,0:T(8,128)S(1)}, f32[128,2560]{1,0:T(8,128)}, u32[]{:S(2)}) copy-start(f32[128,2560]{1,0:T(8,128)} %fusion.95) | copy-start | bytes 3932164
  702.4 21.1 %collective-permute-start.3 = (bf16[128,960]{0,1:T(8,128)(2,1)S(1)}, bf16[128,960]{0,1:T(8,128)(2,1)S(1)}, u32[]{:S(2)}, u32[]{:S(2)}) collective-permute-start(bf16[128,960]{0,1:T(8,128)(2,1)S(1)} %get-tuple-element.677), channel_id=1, source_target_pairs={{16,0},{17,1},{18,2},{19,3},{20,4},{21,5},{22,6},{23,7},{24,8},{25... | collective-permute-start | bytes 737288 | tf_op jit(solution)/shard_map/ppermute | solution.py:23
  703.9 25.1 %slice-start.4 = ((s8[4915200]{0:T(1024)(128)(4,1)}), s8[4194304]{0:T(1024)(128)(4,1)S(1)}, s32[]{:S(2)}) async-start(s8[4915200]{0:T(1024)(128)(4,1)} %bitcast.1125), calls=%async_computation.30 | async-start | bytes 8388608
  748.9 31.2 %copy-start.48 = (f32[128,64]{0,1:T(8,128)S(1)}, f32[128,64]{0,1:T(8,128)}, u32[]{:S(2)}) copy-start(f32[128,64]{0,1:T(8,128)} %copy-done.42) | copy-start | bytes 98308
  748.9 33.7 %copy-start.77 = (bf16[128,960]{0,1:T(8,128)(2,1)S(1)}, bf16[128,960]{0,1:T(8,128)(2,1)}, u32[]{:S(2)}) copy-start(bf16[128,960]{0,1:T(8,128)(2,1)} %copy-done.76) | copy-start | bytes 737284
  751.1 127.3 %reduce-scatter.37.cloned.1.call-start = ((), (), s32[]{:S(2)}) async-start(), calls=%async_computation.20 | async-start | bytes 921600
  752.5 34.9 %copy-start.50 = (bf16[128,960]{0,1:T(8,128)(2,1)S(1)}, bf16[128,960]{0,1:T(8,128)(2,1)}, u32[]{:S(2)}) copy-start(bf16[128,960]{0,1:T(8,128)(2,1)} %copy-done.49) | copy-start | bytes 737284
  787.4 92.7 %reduce-scatter.39.cloned.1.call-start = ((), (), s32[]{:S(2)}) async-start(), calls=%async_computation.21 | async-start | bytes 921600
  798.4 132.4 %reduce-scatter.41.cloned.1.call-start = ((), (), s32[]{:S(2)}) async-start(), calls=%async_computation.22 | async-start | bytes 6553600
  820.9 206.5 %reduce-scatter.43.cloned.1.call-start = ((), (), s32[]{:S(2)}) async-start(), calls=%async_computation.23 | async-start | bytes 6553600
  844.7 279.2 %reduce-scatter.45.cloned.1.call-start = ((), (), s32[]{:S(2)}) async-start(), calls=%async_computation.24 | async-start | bytes 6553600
  868.0 300.8 %reduce-scatter.27.cloned.1.call-start = ((), (), s32[]{:S(2)}) async-start(), calls=%async_computation.10 | async-start | bytes 2457600 | tf_op jit(solution)/shard_map/reduce_scatter | solution.py:366
  873.5 338.8 %reduce-scatter.29.cloned.1.call-start = ((), (), s32[]{:S(2)}) async-start(), calls=%async_computation.11 | async-start | bytes 2457600 | tf_op jit(solution)/shard_map/reduce_scatter | solution.py:375
  878.3 455.9 %all-reduce.10.cloned.1.call-start = ((), (), s32[]{:S(2)}) async-start(), calls=%async_computation.25 | async-start | bytes 9994240 | tf_op jit(solution)/shard_map/psum | solution.py:395
  1126.4 88.8 %copy-start.96 = (bf16[128,960]{0,1:T(8,128)(2,1)S(1)}, bf16[128,960]{0,1:T(8,128)(2,1)}, u32[]{:S(2)}) copy-start(bf16[128,960]{0,1:T(8,128)(2,1)} %copy-done.95) | copy-start | bytes 737284
  1126.4 88.8 %copy-start.127 = (bf16[128,960]{0,1:T(8,128)(2,1)S(1)}, bf16[128,960]{0,1:T(8,128)(2,1)}, u32[]{:S(2)}) copy-start(bf16[128,960]{0,1:T(8,128)(2,1)} %get-tuple-element.772) | copy-start | bytes 737284
  1230.4 24.6 %copy-start.62 = (f32[128,960]{0,1:T(8,128)S(1)}, f32[128,960]{0,1:T(8,128)}, u32[]{:S(2)}) copy-start(f32[128,960]{0,1:T(8,128)} %copy-done.60) | copy-start | bytes 1474564
  1230.4 24.6 %copy-start.181 = (f32[128]{0:T(128)S(1)}, f32[128]{0:T(128)}, u32[]{:S(2)}) copy-start(f32[128]{0:T(128)} %get-tuple-element.745) | copy-start | bytes 1540
  (170 other events, 904.3 us)
Sparse Core Ops, SparseCore 0:
  9.6 67.4 all-gather.14
  78.6 65.8 all-gather.16
  146.0 91.2 all-gather.18
  238.8 91.0 all-gather.22
  331.2 91.0 all-gather.20
  586.0 23.1 reduce-scatter.30
  667.9 25.6 reduce-scatter.32
  751.2 25.6 reduce-scatter.34
  787.5 23.0 reduce-scatter.36
  813.3 22.1 reduce-scatter.38
  837.9 92.9 reduce-scatter.40
  933.0 94.2 reduce-scatter.42
  1029.6 94.2 reduce-scatter.44
  1126.7 42.0 reduce-scatter.26
  1171.6 40.6 reduce-scatter.28
  1217.5 116.7 all-reduce.9
where the time goes:
time: 1360 us; the launch traced here: 1350 us
  waiting for transfers between devices  690 us (51%)
  blocking collectives  249 us (18%)
  matrix products  233 us (17%)
  local copies, waits for them, and re-layouts  91.5 us (7%)
  other arithmetic  60.3 us (4%)
  between operations  21.3 us (2%)
    unnamed x24, waiting for transfers between devices  290 us
    all_gather x1, waiting for transfers between devices, body(): lax.all_gather(w_up[0], 'dp', axis=1, tiled=True)  92.5 us
    all_gather x1, waiting for transfers between devices, body(): lax.all_gather(w_down[0], 'dp', axis=0, tiled=True)  87.9 us
    psum x1, waiting for transfers between devices, body(): lax.psum(shards[0].astype(jnp.bfloat16), 'ctx').astype(jnp.float32)  78.3 us
    unnamed x381, local copies, waits for them, and re-layouts  57 us
    all_gather x1, waiting for transfers between devices, body(): lax.all_gather(w_gate[0], 'dp', axis=1, tiled=True)  54.6 us
    all_gather x1, blocking collectives, body(): lax.all_gather(w_key[0], 'dp', axis=0, tiled=True)  53.7 us
    all_gather x1, blocking collectives, body(): lax.all_gather(w_value[0], 'dp', axis=0, tiled=True)  47.1 us
  transfers between devices with their start and end apart: 20, of which 12 were waited for; matrix products, arithmetic and copies ran while one was open for 14% of the time, Pallas kernels for 0%

commit v1 on v0

v1 whole, which is shorter than its diff:
```python
import jax
import jax.numpy as jnp
from jax import lax
from jax.sharding import PartitionSpec as P

D = 960
HEADS = 15
KV_HEADS = 5
HEAD_DIM = 64
QW = 960
KVW = 320
GROUP = 3
EPSILON = 1e-05
ROPE_BASE = 10000.0
MASKED = -1e30
BF = jnp.bfloat16
F32 = jnp.float32


def dot(a, b):
    return jnp.dot(a, b, preferred_element_type=F32)


def rope_tables(positions):
    half_dim = HEAD_DIM // 2
    freq_rows = ROPE_BASE ** (-(jnp.arange(half_dim, dtype=F32) * 2.0 / HEAD_DIM))
    angles = positions.astype(F32)[:, None] * freq_rows[None, :]
    cosine = jnp.concatenate([jnp.cos(angles), jnp.cos(angles)], axis=1)
    sine_rows = jnp.concatenate([jnp.sin(angles), jnp.sin(angles)], axis=1)
    return (cosine, sine_rows)


def turn_half(u):
    half_dim = HEAD_DIM // 2
    return jnp.concatenate([-u[..., half_dim:], u[..., :half_dim]], axis=-1)


def rotate(u, cosine, sine_rows):
    return u * cosine[:, None, :] + turn_half(u) * sine_rows[:, None, :]


def unrotate(u, cosine, sine_rows):
    return u * cosine[:, None, :] - turn_half(u * sine_rows[:, None, :])


def normalize(x, gain):
    inverse = lax.rsqrt(jnp.mean(x * x, axis=-1, keepdims=True) + EPSILON)
    return (x * inverse * gain, inverse)


def normalize_back(x, inverse, gain, grad):
    scaled = grad * gain
    gain_grad = jnp.sum(grad * x * inverse, axis=0)
    value_grad = inverse * scaled - x * inverse**3 * jnp.mean(scaled * x, axis=-1, keepdims=True)
    return (value_grad, gain_grad)


def attend(q, k, v, query_pos):
    tok = q.shape[0]
    q = q.reshape(tok, KV_HEADS, GROUP, HEAD_DIM)
    scores = jnp.einsum("tkgd,skd->kgts", q, k, preferred_element_type=F32) * HEAD_DIM**-0.5
    allowed = query_pos[:, None] >= jnp.arange(k.shape[0], dtype=jnp.int32)[None, :]
    scores = jnp.where(allowed, scores, MASKED)
    peak = jnp.max(scores, axis=-1, keepdims=True)
    e = jnp.exp(scores - peak)
    total = jnp.sum(e, axis=-1, keepdims=True)
    probs = (e / total).astype(BF)
    o = jnp.einsum("kgts,skd->tkgd", probs, v, preferred_element_type=F32).reshape(tok, QW)
    return o.astype(BF), (peak + jnp.log(total))[..., 0]


def attend_back(q, k, v, lse, do, o, query_pos):
    tok = q.shape[0]
    q = q.reshape(tok, KV_HEADS, GROUP, HEAD_DIM)
    dor = do.reshape(tok, KV_HEADS, GROUP, HEAD_DIM)
    delta = jnp.sum((do.astype(F32) * o.astype(F32)).reshape(tok, KV_HEADS, GROUP, HEAD_DIM), axis=-1)
    delta = jnp.transpose(delta, (1, 2, 0))
    scale = HEAD_DIM**-0.5
    scores = jnp.einsum("tkgd,skd->kgts", q, k, preferred_element_type=F32) * scale
    allowed = query_pos[:, None] >= jnp.arange(k.shape[0], dtype=jnp.int32)[None, :]
    probs = jnp.where(allowed, jnp.exp(scores - lse[..., None]), 0.0)
    dv = jnp.einsum("kgts,tkgd->skd", probs.astype(BF), dor, preferred_element_type=F32)
    dp = jnp.einsum("tkgd,skd->kgts", dor, v, preferred_element_type=F32)
    ds = (probs * (dp - delta[..., None])).astype(BF)
    dq = jnp.einsum("kgts,skd->tkgd", ds, k, preferred_element_type=F32) * scale
    dk = jnp.einsum("kgts,tkgd->skd", ds, q, preferred_element_type=F32) * scale
    dkv = jnp.concatenate([dk.reshape(-1, KVW), dv.reshape(-1, KVW)], axis=1)
    return dq.reshape(tok, HEADS, HEAD_DIM), dkv


def layer_forward(x, w, cosine, sine, query_pos):
    wa, wg, wu, wd, ga, gf = w
    tok = x.shape[0]
    n1, r1 = normalize(x, ga)
    n1 = n1.astype(BF)
    qkv = dot(n1, wa[:, : QW + 2 * KVW])
    q = rotate(qkv[:, :QW].reshape(tok, HEADS, HEAD_DIM), cosine, sine).astype(BF)
    k = rotate(qkv[:, QW : QW + KVW].reshape(tok, KV_HEADS, HEAD_DIM), cosine, sine)
    kv = jnp.concatenate([k.reshape(tok, KVW), qkv[:, QW + KVW :]], axis=1).astype(BF)
    kv = lax.all_gather(kv, "ctx", axis=0, tiled=True)
    k = kv[:, :KVW].reshape(-1, KV_HEADS, HEAD_DIM)
    v = kv[:, KVW:].reshape(-1, KV_HEADS, HEAD_DIM)
    o, lse = attend(q, k, v, query_pos)
    h1 = x + dot(o, wa[:, QW + 2 * KVW :])
    n2, r2 = normalize(h1, gf)
    n2 = lax.all_gather(n2.astype(BF), "dp", axis=0, tiled=True)
    gate = dot(n2, wg)
    up = dot(n2, wu)
    hidden = (jax.nn.silu(gate) * up).astype(BF)
    part = dot(hidden, wd).astype(BF)
    out = h1 + lax.psum_scatter(part, "dp", scatter_dimension=0, tiled=True).astype(F32)
    return out, (x, n1, r1, q, k, v, o, lse, h1, n2, r2, gate, up, hidden)


def layer_backward(g, kept, w, cosine, sine, query_pos):
    wa, wg, wu, wd, ga, gf = w
    x, n1, r1, q, k, v, o, lse, h1, n2, r2, gate, up, hidden = kept
    tok = x.shape[0]
    gb = lax.all_gather(g.astype(BF), "dp", axis=0, tiled=True)
    grad_down = dot(hidden.T, gb)
    dh = dot(gb, wd.T)
    sigma = jax.nn.sigmoid(gate)
    dgate = (dh * up * sigma * (1.0 + gate * (1.0 - sigma))).astype(BF)
    dup = (dh * gate * sigma).astype(BF)
    grad_gate = dot(n2.T, dgate)
    grad_up = dot(n2.T, dup)
    part = (dot(dgate, wg.T) + dot(dup, wu.T)).astype(BF)
    dn2 = lax.psum_scatter(part, "dp", scatter_dimension=0, tiled=True).astype(F32)
    back_f, gain_f = normalize_back(h1, r2, gf, dn2)
    dh1 = g + back_f
    db = dh1.astype(BF)
    grad_out = dot(o.T, db)
    do = dot(db, wa[:, QW + 2 * KVW :].T).astype(BF)
    dq, dkv = attend_back(q, k, v, lse, do, o, query_pos)
    dkv = lax.psum_scatter(dkv.astype(BF), "ctx", scatter_dimension=0, tiled=True).astype(F32)
    dq = unrotate(dq, cosine, sine).reshape(tok, QW)
    dk = unrotate(dkv[:, :KVW].reshape(tok, KV_HEADS, HEAD_DIM), cosine, sine).reshape(tok, KVW)
    dqkv = jnp.concatenate([dq, dk, dkv[:, KVW:]], axis=1).astype(BF)
    grad_qkv = dot(n1.T, dqkv)
    dn1 = dot(dqkv, wa[:, : QW + 2 * KVW].T)
    back_a, gain_a = normalize_back(x, r1, ga, dn1)
    grads = (
        jnp.concatenate([grad_qkv, grad_out], axis=1).astype(BF),
        jnp.stack([gain_a, gain_f]),
        grad_gate.astype(BF),
        grad_up.astype(BF),
        grad_down.astype(BF),
    )
    return dh1 + back_a, grads


def swap_section(p0, p1, section_id):
    mine = jnp.where(section_id == 0, p0, p1)
    other = jnp.where(section_id == 0, p1, p0)
    count = lax.axis_size("section")
    got = lax.ppermute(other, "section", [(i, count - 1 - i) for i in range(count)])
    return mine.astype(F32) + got.astype(F32)


def own_layer(p0, p1, section_id):
    mine = jnp.where(section_id == 0, p0, p1)
    other = jnp.where(section_id == 0, p1, p0)
    count = lax.axis_size("section")
    got = lax.ppermute(other, "section", [(i, count - 1 - i) for i in range(count)])
    first = jnp.where(section_id == 0, mine, got)
    second = jnp.where(section_id == 0, got, mine)
    return jnp.stack([first, second])


def body(
    block_input, out_grad, w_query, w_key, w_value, w_out, norm_attn, w_gate, w_up, w_down, norm_ffn
):
    section_id = lax.axis_index("section")
    tok_rows = block_input.shape[2]
    query_pos = lax.axis_index("ctx") * tok_rows + jnp.arange(tok_rows, dtype=jnp.int32)
    cosine, sine = rope_tables(query_pos)
    x = lax.dynamic_index_in_dim(block_input[:, 0], section_id, 0, keepdims=False)
    g = lax.dynamic_index_in_dim(out_grad[:, 0], section_id, 0, keepdims=False)
    wa = jnp.concatenate([w_query[0], w_key[0], w_value[0], w_out[0]], axis=1)
    wa = lax.all_gather(lax.all_gather(wa, "dp", axis=0, tiled=True), "section")
    gains = jnp.stack([norm_attn[0], norm_ffn[0]])
    gains = lax.all_gather(lax.all_gather(gains, "dp", axis=1, tiled=True), "section").astype(F32)
    wg = lax.all_gather(w_gate[0], "section")
    wu = lax.all_gather(w_up[0], "section")
    wd = lax.all_gather(w_down[0], "section")
    layers = [(wa[l], wg[l], wu[l], wd[l], gains[l, 0], gains[l, 1]) for l in range(2)]
    out0, kept0 = layer_forward(x, layers[0], cosine, sine, query_pos)
    out1, kept1 = layer_forward(out0, layers[1], cosine, sine, query_pos)
    in1, grads1 = layer_backward(g, kept1, layers[1], cosine, sine, query_pos)
    in0, grads0 = layer_backward(in1, kept0, layers[0], cosine, sine, query_pos)
    section_outs = own_layer(out0, out1, section_id)
    in_grads = own_layer(in0, in1, section_id)
    ga, gn, gg, gu, gd = (
        swap_section(a, b, section_id) for a, b in zip(grads0, grads1)
    )
    ga = lax.psum_scatter(ga.astype(BF), "dp", scatter_dimension=0, tiled=True)
    ga = lax.psum(ga, "ctx").astype(F32)
    gn = lax.psum_scatter(gn, "dp", scatter_dimension=1, tiled=True)
    gn = lax.psum(gn, "ctx")
    gg = lax.psum(gg.astype(BF), "ctx").astype(F32)
    gu = lax.psum(gu.astype(BF), "ctx").astype(F32)
    gd = lax.psum(gd.astype(BF), "ctx").astype(F32)
    return (
        section_outs[None, :, None],
        in_grads[None, :, None],
        ga[None, :, :QW],
        ga[None, :, QW : QW + KVW],
        ga[None, :, QW + KVW : QW + 2 * KVW],
        ga[None, :, QW + 2 * KVW :],
        gn[None, 0],
        gg[None],
        gu[None],
        gd[None],
        gn[None, 1],
    )


def solution(mesh):
    return jax.shard_map(
        body,
        mesh=mesh,
        in_specs=(
            P(None, "dp", "ctx", None),
            P(None, "dp", "ctx", None),
            P("section", "dp", None),
            P("section", "dp", None),
            P("section", "dp", None),
            P("section", "dp", None),
            P("section", "dp"),
            P("section", None, "dp"),
            P("section", None, "dp"),
            P("section", "dp", None),
            P("section", "dp"),
        ),
        out_specs=(
            P("section", None, "dp", "ctx", None),
            P("section", None, "dp", "ctx", None),
            P("section", "dp", None),
            P("section", "dp", None),
            P("section", "dp", None),
            P("section", "dp", None),
            P("section", "dp"),
            P("section", None, "dp"),
            P("section", None, "dp"),
            P("section", "dp", None),
            P("section", "dp"),
        ),
        check_vma=False,
    )
```

time: 1360 us -> 742 us (0.55)
  waiting for transfers between devices: 690 us -> 413 us
  matrix products: 233 us -> 78.9 us
  blocking collectives: 249 us -> 138 us
  local copies, waits for them, and re-layouts: 91.5 us -> 44.3 us
  other arithmetic: 60.3 us -> 39.9 us
    unnamed x24 -> x21, waiting for transfers between devices: 290 us -> 125 us
    dot_general x99 -> x42, matrix products: 233 us -> 78.9 us  [the longest x30 62.6 us: dot(): return jnp.dot(a, b, preferred_element_type=F32)]
    all_gather x5, waiting for transfers between devices: 235 us -> 104 us  [the longest x2 104 us: body(): wa = lax.all_gather(lax.all_gather(wa, 'dp', axis=0, tiled=True), 'section')]
    all_gather x14 -> x8, blocking collectives: 216 us -> 128 us  [the longest x2 55.5 us: layer_backward(): gb = lax.all_gather(g.astype(BF), 'dp', axis=0, tiled=True)]
    psum x1, waiting for transfers between devices: 78.3 us -> 106 us  [body(): ga = lax.psum(ga, 'ctx').astype(F32)]
    unnamed x2 -> x0, blocking collectives: 23.5 us -> none
    unnamed x381 -> x251, local copies, waits for them, and re-layouts: 57 us -> 34.5 us
    reduce_scatter x2 -> x1, waiting for transfers between devices: 85.9 us -> 68.9 us  [body(): ga = lax.psum_scatter(ga.astype(BF), 'dp', scatter_dimension=0, tiled=True)]
  transfers between devices with their start and end apart: 20 -> 21, of which waited for: 12 -> 12; matrix products, arithmetic and copies ran while one was open for 14% -> 10% of each run, Pallas kernels for 0% -> 0%
where the time goes in v1:
time: 742 us; the launch traced here: 732 us
  waiting for transfers between devices  413 us (56%)
  blocking collectives  138 us (19%)
  matrix products  78.9 us (11%)
  local copies, waits for them, and re-layouts  44.3 us (6%)
  other arithmetic  39.9 us (5%)
  between operations  16.2 us (2%)
    unnamed x21, waiting for transfers between devices  125 us
    psum x1, waiting for transfers between devices, body(): ga = lax.psum(ga, 'ctx').astype(F32)  106 us
    all_gather x2, waiting for transfers between devices, body(): wa = lax.all_gather(lax.all_gather(wa, 'dp', axis=0, tiled=True), 'section')  104 us
    reduce_scatter x1, waiting for transfers between devices, body(): ga = lax.psum_scatter(ga.astype(BF), 'dp', scatter_dimension=0, tiled=True)  68.9 us
    dot_general x30, matrix products, dot(): return jnp.dot(a, b, preferred_element_type=F32)  62.6 us
    all_gather x2, blocking collectives, layer_backward(): gb = lax.all_gather(g.astype(BF), 'dp', axis=0, tiled=True)  55.5 us
    all_gather x2, blocking collectives, layer_forward(): n2 = lax.all_gather(n2.astype(BF), 'dp', axis=0, tiled=True)  40.4 us
    unnamed x251, local copies, waits for them, and re-layouts  34.5 us
  transfers between devices with their start and end apart: 21, of which 12 were waited for; matrix products, arithmetic and copies ran while one was open for 10% of the time, Pallas kernels for 0%

profile of v1, /device:TPU:0, one launch (start us, length us, event | category | flops | bytes accessed | tf_op | source)
XLA Modules:
  0.0 732.5 jit_solution(13882439733728166698)
XLA Ops:
  9.4 3.4 concatenate.83
  12.9 95.5 %all-gather.10.cloned.1.call-done = bf16[960,2560]{1,0:T(8,128)(2,1)} async-done(((bf16[240,2560]{1,0:T(8,128)(2,1)}), bf16[960,2560]{1,0:T(8,128)(2,1)}) %all-gather.10.cloned.1.call-update) | async-done | bytes 4915216 | tf_op jit(solution)/shard_map/all_gather | solution.py:180
  110.4 8.1 %all-gather.2 = bf16[4,240,2]{1,2,0:T(2,128)(2,1)S(1)} all-gather(bf16[1,240,2]{1,2,0:T(2,128)(2,1)S(1)} %maximum_bitcast_fusion.2), channel_id=1, replica_groups=mesh['section'=2,'ctx'=4,'dp'=4] {'dp'}, dimensions={0}, use_global_device_ids=true | all-gather | bytes 4800 | tf_op jit(solution)/shard_map/all_gather | solution.py:182
  118.6 1.8 all-gather.3
  121.4 8.9 %all-gather.18.cloned.1.call-done = bf16[1920,2560]{1,0:T(8,128)(2,1)} async-done(((bf16[960,2560]{1,0:T(8,128)(2,1)}), bf16[1920,2560]{1,0:T(8,128)(2,1)}) %all-gather.18.cloned.1.call-update) | async-done | bytes 9830416 | tf_op jit(solution)/shard_map/all_gather | solution.py:180
  130.3 3.5 fusion.20
  134.0 11.5 %all_gather.51 = bf16[512,640]{0,1:T(8,128)(2,1)S(1)} all-gather(bf16[128,640]{0,1:T(8,128)(2,1)S(1)} %pad_maximum_fusion.12), channel_id=1, replica_groups=mesh['section'=2,'ctx'=4,'dp'=4] {'ctx'}, dimensions={0}, use_global_device_ids=true | all-gather | bytes 819200 | tf_op jit(solution)/shard_map/all_gather | solution.py:100
  148.5 3.6 multiply_reduce_fusion.4
  152.9 20.9 %all_gather.52 = bf16[512,960]{0,1:T(8,128)(2,1)S(1)} all-gather(bf16[128,960]{0,1:T(8,128)(2,1)S(1)} %multiply_convert_fusion.8), channel_id=1, replica_groups=mesh['section'=2,'ctx'=4,'dp'=4] {'dp'}, dimensions={0}, use_global_device_ids=true | all-gather | bytes 1228800 | tf_op jit(solution)/shard_map/all_gather | solution.py:106
  173.8 3.7 fusion.72
  177.5 3.8 multiply_convert_fusion.5
  181.3 2.5 convolution_convert_fusion.11
  186.2 34.5 %all_gather.58 = bf16[512,960]{0,1:T(8,128)(2,1)S(1)} all-gather(bf16[128,960]{0,1:T(8,128)(2,1)S(1)} %bitcast_convert_fusion), channel_id=1, replica_groups=mesh['section'=2,'ctx'=4,'dp'=4] {'dp'}, dimensions={0}, use_global_device_ids=true | all-gather | bytes 1228800 | tf_op jit(solution)/shard_map/all_gather | solution.py:119
  220.7 2.0 reduce-scatter.25.cloned.1.call-done
  224.6 3.5 fusion.16
  228.2 10.9 %all_gather.56 = bf16[512,640]{0,1:T(8,128)(2,1)S(1)} all-gather(bf16[128,640]{0,1:T(8,128)(2,1)S(1)} %pad_maximum_fusion.13), channel_id=1, replica_groups=mesh['section'=2,'ctx'=4,'dp'=4] {'ctx'}, dimensions={0}, use_global_device_ids=true | all-gather | bytes 819200 | tf_op jit(solution)/shard_map/all_gather | solution.py:100
  242.9 3.7 multiply_reduce_fusion.2
  246.8 19.6 %all_gather.57 = bf16[512,960]{0,1:T(8,128)(2,1)S(1)} all-gather(bf16[128,960]{0,1:T(8,128)(2,1)S(1)} %multiply_convert_fusion.6), channel_id=1, replica_groups=mesh['section'=2,'ctx'=4,'dp'=4] {'dp'}, dimensions={0}, use_global_device_ids=true | all-gather | bytes 1228800 | tf_op jit(solution)/shard_map/all_gather | solution.py:106
  270.1 2.3 multiply_convert_fusion.2
  276.1 2.2 convolution_convert_fusion.10
  279.8 22.0 %reduce-scatter.29.cloned.1.call-done = bf16[128,960]{1,0:T(8,128)(2,1)} async-done(((bf16[512,960]{1,0:T(8,128)(2,1)}), bf16[128,960]{1,0:T(8,128)(2,1)}) %reduce-scatter.29.cloned.1.call-update) | async-done | bytes 245776
  305.1 3.3 convert_multiply_fusion.5
  308.4 3.8 fusion.3
  315.0 2.2 copy.88
  318.9 10.9 %reduce-scatter.27.cloned.1.call-done = bf16[128,960]{1,0:T(8,128)(2,1)} async-done(((bf16[512,960]{1,0:T(8,128)(2,1)}), bf16[128,960]{1,0:T(8,128)(2,1)}) %reduce-scatter.27.cloned.1.call-update) | async-done | bytes 245776
  331.0 26.6 %reduce-scatter.31.cloned.1.call-done = bf16[128,640]{1,0:T(8,128)(2,1)} async-done(((bf16[512,640]{1,0:T(8,128)(2,1)}), bf16[128,640]{1,0:T(8,128)(2,1)}) %reduce-scatter.31.cloned.1.call-update) | async-done | bytes 163856
  359.1 3.7 multiply_reduce_fusion
  363.9 21.0 %all_gather.59 = bf16[512,960]{0,1:T(8,128)(2,1)S(1)} all-gather(bf16[128,960]{0,1:T(8,128)(2,1)S(1)} %get-tuple-element.58), channel_id=1, replica_groups=mesh['section'=2,'ctx'=4,'dp'=4] {'dp'}, dimensions={0}, use_global_device_ids=true | all-gather | bytes 1228800 | tf_op jit(solution)/shard_map/all_gather | solution.py:119
  391.3 2.0 convolution_convert_fusion.2
  393.2 23.6 %reduce-scatter.33.cloned.1.call-done = bf16[128,960]{1,0:T(8,128)(2,1)} async-done(((bf16[512,960]{1,0:T(8,128)(2,1)}), bf16[128,960]{1,0:T(8,128)(2,1)}) %reduce-scatter.33.cloned.1.call-update) | async-done | bytes 245776
  419.1 2.6 convert_multiply_fusion.4
  421.8 3.1 fusion.54
  429.7 2.4 convolution_convert_fusion
  433.9 1.9 convolution_convert_fusion.3
  435.9 18.0 %reduce-scatter.35.cloned.1.call-done = bf16[128,640]{1,0:T(8,128)(2,1)} async-done(((bf16[512,640]{1,0:T(8,128)(2,1)}), bf16[128,640]{1,0:T(8,128)(2,1)}) %reduce-scatter.35.cloned.1.call-update) | async-done | bytes 163856
  453.9 1.7 fusion.143
  461.4 2.2 convolution_convert_fusion.1
  463.7 5.0 broadcast_select_fusion
  468.8 8.2 %collective-permute-done.2 = bf16[960,2560]{1,0:T(8,128)(2,1)S(1)} collective-permute-done((bf16[960,2560]{1,0:T(8,128)(2,1)S(1)}, bf16[960,2560]{1,0:T(8,128)(2,1)S(1)}, u32[]{:S(2)}, u32[]{:S(2)}) %collective-permute-start.2) | collective-permute-done | bytes 4915232 | tf_op jit(solution)/shard_map/ppermute | solution.py:156
  477.0 6.3 add_convert_fusion
  491.7 2.0 broadcast_select_fusion.1
  495.4 1.8 fusion.109
  500.3 2.8 fusion.48
  503.1 68.9 %reduce-scatter.23.cloned.1.call-done = bf16[240,2560]{1,0:T(8,128)(2,1)} async-done(((bf16[960,2560]{1,0:T(8,128)(2,1)}), bf16[240,2560]{1,0:T(8,128)(2,1)}) %reduce-scatter.23.cloned.1.call-update) | async-done | bytes 1228816 | tf_op jit(solution)/shard_map/reduce_scatter | solution.py:196
  573.3 2.0 broadcast_select_fusion.4
  576.6 20.3 %reduce-scatter.37.cloned.1.call-done = f32[240,2]{1,0:T(8,128)} async-done(((f32[960,2]{1,0:T(8,128)}), f32[240,2]{1,0:T(8,128)}) %reduce-scatter.37.cloned.1.call-update) | async-done | bytes 1936
  597.9 9.8 %psum.36 = f32[2,240]{1,0:T(2,128)S(1)} all-reduce(f32[2,240]{1,0:T(2,128)S(1)} %copy.95), channel_id=1, replica_groups=mesh['section'=2,'ctx'=4,'dp'=4] {'ctx'}, use_global_device_ids=true, to_apply=%region_27.28 | all-reduce | flops 480 | bytes 3840 | tf_op jit(solution)/shard_map/psum | solution.py:199
  609.4 106.0 %all-reduce.3.cloned.1.call-done = (bf16[240,2560]{1,0:T(8,128)(2,1)}, bf16[1,960,640]{2,1,0:T(8,128)(2,1)}, bf16[1,960,640]{2,1,0:T(8,128)(2,1)}, bf16[1,640,960]{1,2,0:T(8,128)(2,1)}) async-done(((bf16[240,2560]{1,0:T(8,128)(2,1)}, bf16[1,960,640]{2,1,0:T(8,128)(2,1)}, bf16[1,960,640]{2,1,0:T(8,128)(2,1)}, bf16[1,640,960]{1,2,0:T(8,128)(2,1)}), (bf16[240,2560]{1,0:T(8,128)(2,1)}, ...) | async-done | bytes 4915216 | tf_op jit(solution)/shard_map/psum | solution.py:197
  (405 shorter events, 86.7 us)
Async XLA Ops:
  7.2 101.2 %all-gather.10.cloned.1.call-start = ((), (), s32[]{:S(2)}) async-start(), calls=%async_computation.8 | async-start | bytes 6144000 | tf_op jit(solution)/shard_map/all_gather | solution.py:180
  12.8 117.5 %all-gather.18.cloned.1.call-start = ((), (), s32[]{:S(2)}) async-start(), calls=%async_computation.13 | async-start | bytes 14745600 | tf_op jit(solution)/shard_map/all_gather | solution.py:180
  108.4 65.3 %all-gather.12.cloned.1.call-start = ((), (), s32[]{:S(2)}) async-start(), calls=%async_computation.9 | async-start | bytes 3686400 | tf_op jit(solution)/shard_map/all_gather | solution.py:183
  109.1 68.3 %all-gather.14.cloned.1.call-start = ((), (), s32[]{:S(2)}) async-start(), calls=%async_computation.10 | async-start | bytes 3686400 | tf_op jit(solution)/shard_map/all_gather | solution.py:184
  109.7 71.6 %all-gather.16.cloned.1.call-start = ((), (), s32[]{:S(2)}) async-start(), calls=%async_computation.11 | async-start | bytes 3686400 | tf_op jit(solution)/shard_map/all_gather | solution.py:185
  110.3 112.4 %reduce-scatter.25.cloned.1.call-start = ((), (), s32[]{:S(2)}) async-start(), calls=%async_computation.14 | async-start | bytes 1310720
  120.4 32.3 %copy-start.87 = (f32[1,1,960]{2,1,0:T(1,128)}, f32[1,1,960]{2,1,0:T(1,128)S(1)}, u32[]{:S(2)}) copy-start(f32[1,1,960]{2,1,0:T(1,128)S(1)} %get-tuple-element.102) | copy-start | bytes 11524
  120.4 104.1 %copy-start.82 = (f32[1,1,960]{2,1,0:T(1,128)}, f32[1,1,960]{2,1,0:T(1,128)S(1)}, u32[]{:S(2)}) copy-start(f32[1,1,960]{2,1,0:T(1,128)S(1)} %get-tuple-element.101) | copy-start | bytes 11524
  121.3 237.6 %copy-start.26 = (f32[128,64]{0,1:T(8,128)}, f32[128,64]{0,1:T(8,128)S(1)}, u32[]{:S(2)}) copy-start(f32[128,64]{0,1:T(8,128)S(1)} %pad_maximum_fusion.17) | copy-start | bytes 98308
  121.4 120.3 %copy-start.45 = (pred[128,512]{0,1:T(8,128)(4,1)}, pred[128,512]{0,1:T(8,128)(4,1)S(1)}, u32[]{:S(2)}) copy-start(pred[128,512]{0,1:T(8,128)(4,1)S(1)} %iota_compare_fusion) | copy-start | bytes 196612
  148.5 25.2 %copy-start.58 = (bf16[5,64,3,128]{3,1,2,0:T(8,128)(2,1)}, bf16[5,64,3,128]{3,1,2,0:T(8,128)(2,1)S(1)}, u32[]{:S(2)}) copy-start(bf16[5,64,3,128]{3,1,2,0:T(8,128)(2,1)S(1)} %fusion.64) | copy-start | bytes 737284
  152.7 24.8 %copy-start.94 = (f32[128]{0:T(128)}, f32[128]{0:T(128)S(1)}, u32[]{:S(2)}) copy-start(f32[128]{0:T(128)S(1)} %get-tuple-element.111) | copy-start | bytes 1540
  185.1 116.6 %reduce-scatter.29.cloned.1.call-start = ((), (), s32[]{:S(2)}) async-start(), calls=%async_computation.16 | async-start | bytes 1310720
  220.7 48.7 %copy-start.21 = (bf16[512,960]{0,1:T(8,128)(2,1)}, bf16[512,960]{0,1:T(8,128)(2,1)S(1)}, u32[]{:S(2)}) copy-start(bf16[512,960]{0,1:T(8,128)(2,1)S(1)} %all_gather.58) | copy-start | bytes 2949124
  224.0 138.9 %copy-start.8 = (f32[128,960]{0,1:T(8,128)}, f32[128,960]{0,1:T(8,128)S(1)}, u32[]{:S(2)}) copy-start(f32[128,960]{0,1:T(8,128)S(1)} %get-tuple-element.61) | copy-start | bytes 1474564
  242.9 23.5 %copy-start.35 = (bf16[2,960,640]{2,1,0:T(8,128)(2,1)S(1)}, bf16[2,960,640]{2,1,0:T(8,128)(2,1)}, u32[]{:S(2)}) copy-start(bf16[2,960,640]{2,1,0:T(8,128)(2,1)} %all-gather.12.cloned.1.call-done) | copy-start | bytes 7372804
  246.5 116.3 %copy-start.6 = (f32[128,960]{0,1:T(8,128)}, f32[128,960]{0,1:T(8,128)S(1)}, u32[]{:S(2)}) copy-start(f32[128,960]{0,1:T(8,128)S(1)} %get-tuple-element.125) | copy-start | bytes 1474564
  275.9 54.0 %reduce-scatter.27.cloned.1.call-start = ((), (), s32[]{:S(2)}) async-start(), calls=%async_computation.15 | async-start | bytes 1310720
  279.7 25.4 %copy-start.62 = (bf16[5,64,3,128]{3,1,2,0:T(8,128)(2,1)S(1)}, bf16[5,64,3,128]{3,1,2,0:T(8,128)(2,1)}, u32[]{:S(2)}) copy-start(bf16[5,64,3,128]{3,1,2,0:T(8,128)(2,1)} %copy-done.61) | copy-start | bytes 737284
  279.7 77.8 %reduce-scatter.31.cloned.1.call-start = ((), (), s32[]{:S(2)}) async-start(), calls=%async_computation.17 | async-start | bytes 819200
  317.2 99.6 %reduce-scatter.33.cloned.1.call-start = ((), (), s32[]{:S(2)}) async-start(), calls=%async_computation.18 | async-start | bytes 1310720
  318.7 40.2 %copy-start.83 = (f32[1,1,960]{2,1,0:T(1,128)S(1)}, f32[1,1,960]{2,1,0:T(1,128)}, u32[]{:S(2)}) copy-start(f32[1,1,960]{2,1,0:T(1,128)} %copy-done.82) | copy-start | bytes 11524
  318.7 40.2 %copy-start.99 = (f32[128]{0:T(128)S(1)}, f32[128]{0:T(128)}, u32[]{:S(2)}) copy-start(f32[128]{0:T(128)} %copy-done.98) | copy-start | bytes 1540
  318.9 43.9 %copy-start.51 = (bf16[128,960]{0,1:T(8,128)(2,1)}, bf16[128,960]{0,1:T(8,128)(2,1)S(1)}, u32[]{:S(2)}) copy-start(bf16[128,960]{0,1:T(8,128)(2,1)S(1)} %fusion.94) | copy-start | bytes 737284
  331.0 31.9 %copy-start.43 = (bf16[128,960]{0,1:T(8,128)(2,1)}, bf16[128,960]{0,1:T(8,128)(2,1)S(1)}, u32[]{:S(2)}) copy-start(bf16[128,960]{0,1:T(8,128)(2,1)S(1)} %copy.85) | copy-start | bytes 737284
  359.0 25.8 %copy-start.111 = (f32[512,640]{1,0:T(8,128)S(1)}, f32[512,640]{1,0:T(8,128)}, u32[]{:S(2)}) copy-start(f32[512,640]{1,0:T(8,128)} %get-tuple-element.121) | copy-start | bytes 3932164
  362.8 22.1 %copy-start.107 = (bf16[2,640,960]{1,2,0:T(8,128)(2,1)S(1)}, bf16[2,640,960]{1,2,0:T(8,128)(2,1)}, u32[]{:S(2)}) copy-start(bf16[2,640,960]{1,2,0:T(8,128)(2,1)} %all-gather.16.cloned.1.call-done) | copy-start | bytes 7372804
  362.8 22.1 %copy-start.110 = (f32[512,640]{1,0:T(8,128)S(1)}, f32[512,640]{1,0:T(8,128)}, u32[]{:S(2)}) copy-start(f32[512,640]{1,0:T(8,128)} %fusion.72) | copy-start | bytes 3932164
  363.9 55.0 %copy-start.14 = (f32[128,960]{0,1:T(8,128)}, f32[128,960]{0,1:T(8,128)S(1)}, u32[]{:S(2)}) copy-start(f32[128,960]{0,1:T(8,128)S(1)} %get-tuple-element.59) | copy-start | bytes 1474564
  390.9 27.0 %copy-start.88 = (f32[1,1,960]{2,1,0:T(1,128)S(1)}, f32[1,1,960]{2,1,0:T(1,128)}, u32[]{:S(2)}) copy-start(f32[1,1,960]{2,1,0:T(1,128)} %copy-done.87) | copy-start | bytes 11524
  390.9 27.0 %copy-start.95 = (f32[128]{0:T(128)S(1)}, f32[128]{0:T(128)}, u32[]{:S(2)}) copy-start(f32[128]{0:T(128)} %copy-done.94) | copy-start | bytes 1540
  390.9 28.0 %copy-start.103 = (f32[128]{0:T(128)S(1)}, f32[128]{0:T(128)}, u32[]{:S(2)}) copy-start(f32[128]{0:T(128)} %get-tuple-element.110) | copy-start | bytes 1540
  390.9 63.0 %reduce-scatter.35.cloned.1.call-start = ((), (), s32[]{:S(2)}) async-start(), calls=%async_computation.19 | async-start | bytes 819200
  391.3 27.9 %copy-start.59 = (bf16[5,64,3,128]{3,1,2,0:T(8,128)(2,1)S(1)}, bf16[5,64,3,128]{3,1,2,0:T(8,128)(2,1)}, u32[]{:S(2)}) copy-start(bf16[5,64,3,128]{3,1,2,0:T(8,128)(2,1)} %copy-done.58) | copy-start | bytes 737284
  429.6 142.3 %reduce-scatter.23.cloned.1.call-start = ((), (), s32[]{:S(2)}) async-start(), calls=%async_computation.12 | async-start | bytes 6144000 | tf_op jit(solution)/shard_map/reduce_scatter | solution.py:196
  433.0 25.9 %copy-start.28 = (f32[128,64]{0,1:T(8,128)S(1)}, f32[128,64]{0,1:T(8,128)}, u32[]{:S(2)}) copy-start(f32[128,64]{0,1:T(8,128)} %copy-done.26) | copy-start | bytes 98308
  433.9 29.7 %copy-start.52 = (bf16[128,960]{0,1:T(8,128)(2,1)}, bf16[128,960]{0,1:T(8,128)(2,1)S(1)}, u32[]{:S(2)}) copy-start(bf16[128,960]{0,1:T(8,128)(2,1)S(1)} %fusion.96) | copy-start | bytes 737284
  433.9 27.5 %copy-start.81 = (f32[1,1,960]{2,1,0:T(1,128)S(1)}, f32[1,1,960]{2,1,0:T(1,128)}, u32[]{:S(2)}) copy-start(f32[1,1,960]{2,1,0:T(1,128)} %copy-done.80) | copy-start | bytes 11524
  433.9 27.5 %copy-start.97 = (f32[128]{0:T(128)S(1)}, f32[128]{0:T(128)}, u32[]{:S(2)}) copy-start(f32[128]{0:T(128)} %copy-done.96) | copy-start | bytes 1540
  468.8 8.3 %collective-permute-start.2 = (bf16[960,2560]{1,0:T(8,128)(2,1)S(1)}, bf16[960,2560]{1,0:T(8,128)(2,1)S(1)}, u32[]{:S(2)}, u32[]{:S(2)}) collective-permute-start(bf16[960,2560]{1,0:T(8,128)(2,1)S(1)} %broadcast_select_fusion), channel_id=1, source_target_pairs={{0,16},{16,0},{1,17},{17,1},{2,18},{18,2},{3,19},{19,3},{4,20},{20... | collective-permute-start | bytes 14745608 | tf_op jit(solution)/shard_map/ppermute | solution.py:156
  483.3 113.6 %reduce-scatter.37.cloned.1.call-start = ((), (), s32[]{:S(2)}) async-start(), calls=%async_computation.20 | async-start | bytes 614400
  486.6 7.2 collective-permute-start.4
  489.1 8.6 %collective-permute-start.5 = (bf16[960,640]{1,0:T(8,128)(2,1)S(1)}, bf16[960,640]{1,0:T(8,128)(2,1)S(1)}, u32[]{:S(2)}, u32[]{:S(2)}) collective-permute-start(bf16[960,640]{1,0:T(8,128)(2,1)S(1)} %get-tuple-element.134), channel_id=1, source_target_pairs={{0,16},{16,0},{1,17},{17,1},{2,18},{18,2},{3,19},{19,3},{4,20},{20... | collective-permute-start | bytes 3686408 | tf_op jit(solution)/shard_map/ppermute | solution.py:156
  493.6 6.7 collective-permute-start.6
  497.3 1.9 collective-permute-start.3
  500.2 215.2 %all-reduce.3.cloned.1.call-start = ((), (), s32[]{:S(2)}) async-start(), calls=%async_computation.21 | async-start | bytes 9830400 | tf_op jit(solution)/shard_map/psum | solution.py:197
  573.0 2.5 collective-permute-start
  575.3 33.0 %collective-permute-start.1 = (f32[128,960]{0,1:T(8,128)}, f32[128,960]{0,1:T(8,128)S(1)}, u32[]{:S(2)}, u32[]{:S(2)}) collective-permute-start(f32[128,960]{0,1:T(8,128)} %get-tuple-element.56), channel_id=1, source_target_pairs={{0,16},{16,0},{1,17},{17,1},{2,18},{18,2},{3,19},{19,3},{4,20},{20... | collective-permute-start | bytes 1474568 | tf_op jit(solution)/shard_map/ppermute | solution.py:164
  (88 other events, 241.1 us)
Sparse Core Ops, SparseCore 0:
  13.0 95.3 all-gather.9
  109.9 20.3 all-gather.17
  131.9 12.2 all-gather.11
  145.6 12.2 all-gather.13
  159.3 12.2 all-gather.15
  185.2 37.4 reduce-scatter.24
  276.0 25.7 reduce-scatter.28
  304.0 25.7 reduce-scatter.26
  333.3 24.1 reduce-scatter.30
  391.1 25.6 reduce-scatter.32
  429.8 24.1 reduce-scatter.34
  483.4 88.4 reduce-scatter.22
  574.8 22.0 reduce-scatter.36
  601.7 113.6 all-reduce.2
